TPU v7x, 32 devices: a whole 2x2x4 slice. The times are simulated.
32 devices in a mesh: subtree: 4 (over y, core), tile: 8 (over z, x).
Axes of the slice: x: 2, y: 2, z: 4, core: 2. Of those that a mesh axis runs over, the one named last changes fastest.
Arguments:
- interface_stiffness: float32 [4, 4096, 4096], P('subtree', 'tile'), may hold values from -3 to 3
- lower_factor: bfloat16 [4, 4096, 512], P('subtree', 'tile'), may hold values from -0.25 to 0.25
- upper_factor: bfloat16 [4, 512, 4096], P('subtree', None, 'tile'), may hold values from -6 to 6
- modes: bfloat16 [4096, 256], P('tile'), may hold values from -0.09375 to 0.09375
- gyro_rows: int32 [512], replicated, may hold values from 0 to 4095, as said below
- gyro_coupling: float32 [512, 512], replicated, may hold values from -24 to 24
- spin_softening: float32 [512], replicated, may hold values from 0.5 to 8
- speed_index: int32 [2], replicated, may hold values from 0 to 63
Outputs:
- schur: float32 [4096, 4096], P('tile', 'subtree')
- campbell: float32 [2, 256, 256], P(None, 'tile', 'subtree')
Inputs may be any that keep to these rules, and one draw needn't show every extreme that they name: `gyro_rows`: distinct interface degrees of freedom, in whole aligned blocks of 8 consecutive ones.
All inputs are finite; a program needn't handle non-finite values.
Results may differ from a plain program's by a relative error of at most 0.0003.
Values may be sent and summed in bfloat16 or wider, within the bound.
No kernel may reach another device: no remote copies, remote signals or barrier semaphores. Data moves between devices by JAX's collectives and lax.ppermute only.
A program may use at most 64 MiB of HBM per device.

v0:
```python
import jax
import jax.numpy as jnp
from jax import lax
from jax.sharding import PartitionSpec as P

SPEED_STEPS = 64
OMEGA_TOP = 2.0


def partner(block, axis, distance):
    count = lax.axis_size(axis)
    route = []
    for low in range(count):
        high = low | 1 << distance
        if high != low and high < count:
            route += [(low, high), (high, low)]
    return lax.ppermute(block, axis, route)


def shards(
    interface_stiffness,
    lower_factor,
    upper_factor,
    modes,
    gyro_rows,
    gyro_coupling,
    spin_softening,
    speed_index,
):
    tile_count = lax.axis_size("tile")
    branch_count = lax.axis_size("subtree")
    tile_pos = lax.axis_index("tile")
    branch_pos = lax.axis_index("subtree")
    mode_count = modes.shape[1]
    mode_cols = mode_count // branch_count
    mode_rows_dev = mode_count // tile_count
    coupled = jnp.einsum(
        "lrk,lkn->rn",
        lower_factor,
        lax.all_gather(upper_factor, "tile", axis=2, tiled=True),
        preferred_element_type=jnp.float32,
    )
    schur_rows = jnp.sum(interface_stiffness, axis=0) - coupled
    full_width = schur_rows.shape[1]
    own_width = full_width // branch_count
    own_first = branch_pos * own_width
    schur_part = schur_rows
    for level_bit in range(branch_count.bit_length() - 1):
        schur_part = schur_part + partner(schur_part, "subtree", level_bit)
    schur_out = lax.dynamic_slice_in_dim(schur_part, own_first, own_width, 1)
    col_first = branch_pos * mode_cols
    segment = lax.all_gather(modes, "tile", axis=0, tiled=True)
    row_count = segment.shape[0]
    wanted = lax.dynamic_slice_in_dim(segment, col_first, mode_cols, 1).astype(jnp.float32)
    response = jnp.dot(
        schur_part, wanted, precision=lax.Precision.HIGHEST, preferred_element_type=jnp.float32
    )
    inside = (gyro_rows >= 0) & (gyro_rows < row_count)
    taken = jnp.take(segment, jnp.clip(gyro_rows, 0, row_count - 1), axis=0).astype(jnp.float32)
    picked = jnp.where(inside[:, None], taken, jnp.float32(0.0))
    response, picked = (response, picked)
    local_modes = modes.astype(jnp.float32)
    partial_value = jnp.einsum(
        "rm,rc->mc",
        local_modes,
        response,
        precision=lax.Precision.HIGHEST,
        preferred_element_type=jnp.float32,
    )
    stiff_block = lax.psum_scatter(partial_value, "tile", scatter_dimension=0, tiled=True)
    skew_part = 0.5 * (gyro_coupling - gyro_coupling.T)
    left_modes = lax.dynamic_slice_in_dim(picked, tile_pos * mode_rows_dev, mode_rows_dev, 1)
    right_modes = lax.dynamic_slice_in_dim(picked, branch_pos * mode_cols, mode_cols, 1)
    turned = jnp.dot(
        skew_part, right_modes, precision=lax.Precision.HIGHEST, preferred_element_type=jnp.float32
    )
    gyro_block = jnp.einsum(
        "gm,gc->mc",
        left_modes,
        turned,
        precision=lax.Precision.HIGHEST,
        preferred_element_type=jnp.float32,
    )
    spin_block = jnp.einsum(
        "gm,gc->mc",
        left_modes,
        spin_softening[:, None] * right_modes,
        precision=lax.Precision.HIGHEST,
        preferred_element_type=jnp.float32,
    )
    speeds_omega = OMEGA_TOP * (speed_index.astype(jnp.float32) + 1.0) / SPEED_STEPS
    campbell = (
        stiff_block[None]
        + speeds_omega[:, None, None] * gyro_block[None]
        - (speeds_omega * speeds_omega)[:, None, None] * spin_block[None]
    )
    return (schur_out, campbell)


def solution(mesh):
    placed = (
        P("subtree", "tile", None),
        P("subtree", "tile", None),
        P("subtree", None, "tile"),
        P("tile", None),
        P(),
        P(),
        P(),
        P(),
    )
    return jax.shard_map(
        shards,
        mesh=mesh,
        in_specs=placed,
        out_specs=(P("tile", "subtree"), P(None, "tile", "subtree")),
        check_vma=False,
    )
```

profile of v0, /device:TPU:0, one launch (start us, length us, event | category | flops | bytes accessed | tf_op | source)
XLA Modules:
  0.0 391.6 jit_solution(2700897672948704366)
XLA Ops:
  7.2 0.0 copy-start
  7.2 0.0 all-gather.3.cloned.1.call-start
  7.2 0.7 all-gather.3.cloned.1.call-update
  7.9 0.0 all-gather.5.cloned.1.call-start
  8.0 79.8 %all-gather.3.cloned.1.call-done = bf16[1,512,4096]{2,1,0:T(8,128)(2,1)} async-done(((bf16[1,512,512]{2,1,0:T(8,128)(2,1)}), bf16[1,512,4096]{2,1,0:T(8,128)(2,1)}) %all-gather.3.cloned.1.call-update) | async-done | bytes 4194320 | tf_op jit(solution)/shard_map/all_gather | solution.py:40
  87.8 0.0 copy-done
  87.8 7.0 %bitcast_subtract_fusion = f32[512,4096]{1,0:T(8,128)S(1)} fusion(f32[1,512,4096]{2,1,0:T(8,128)} %param.8, bf16[1,512,4096]{2,1,0:T(8,128)(2,1)} %all-gather.3.cloned.1.call-done, bf16[1,512,512]{2,1,0:T(8,128)(2,1)S(1)} %copy-done), kind=kOutput, calls=%fused_computation.1 | convolution fusion | flops 2149580800 | bytes 21495808 | tf_op jit(solution)/shard_map/lrk,lkn->rn/dot_general | solution.py:37
  94.8 0.0 copy-start.1
  94.8 3.2 copy-done.1
  98.1 0.0 copy-start.3
  98.1 0.0 copy-start.5
  98.1 0.0 copy-start.7
  98.1 0.0 copy-start.6
  98.1 0.1 collective-permute-start
  98.2 13.3 %collective-permute-done = f32[512,4096]{1,0:T(8,128)} collective-permute-done((f32[512,4096]{1,0:T(8,128)S(1)}, f32[512,4096]{1,0:T(8,128)}, u32[]{:S(2)}, u32[]{:S(2)}) %collective-permute-start) | collective-permute-done | bytes 8388640 | tf_op jit(solution)/shard_map/ppermute | solution.py:17
  111.4 11.1 %add.35 = f32[512,4096]{1,0:T(8,128)} add(f32[512,4096]{1,0:T(8,128)} %copy-done.1, f32[512,4096]{1,0:T(8,128)} %collective-permute-done) | non-fusion elementwise | flops 2097152 | bytes 25165824 | tf_op jit(solution)/shard_map/add | solution.py:49
  122.6 1.5 collective-permute-start.1
  124.1 0.0 all-gather.5.cloned.1.call-update
  124.1 0.0 reduce-scatter.4.cloned.1.call-start
  124.1 0.0 copy-done.3
  124.2 0.3 copy.13
  124.5 0.0 copy-done.5
  124.5 0.0 copy-done.7
  124.6 46.2 %all-gather.5.cloned.1.call-done = bf16[4096,256]{1,0:T(8,128)(2,1)} async-done(((bf16[512,256]{1,0:T(8,128)(2,1)}), bf16[4096,256]{1,0:T(8,128)(2,1)}) %all-gather.5.cloned.1.call-update) | async-done | bytes 2097168 | tf_op jit(solution)/shard_map/all_gather | solution.py:52
  170.8 3.4 gather_fusion
  174.2 0.2 convert_select_fusion
  174.4 0.0 copy-done.6
  174.4 0.8 fusion.8
  175.3 1.1 fusion.2
  176.4 0.7 fusion.13
  177.0 0.0 copy-start.2
  177.0 128.3 %collective-permute-done.1 = f32[512,4096]{1,0:T(8,128)} collective-permute-done((f32[512,4096]{1,0:T(8,128)}, f32[512,4096]{1,0:T(8,128)}, u32[]{:S(2)}, u32[]{:S(2)}) %collective-permute-start.1) | collective-permute-done | bytes 8388640 | tf_op jit(solution)/shard_map/ppermute | solution.py:17
  305.4 11.1 %add.36 = f32[512,4096]{1,0:T(8,128)} add(f32[512,4096]{1,0:T(8,128)} %add.35, f32[512,4096]{1,0:T(8,128)} %collective-permute-done.1) | non-fusion elementwise | flops 2097152 | bytes 25165824 | tf_op jit(solution)/shard_map/add | solution.py:49
  316.5 0.0 copy-done.2
  316.5 0.0 copy-start.4
  316.5 6.7 %fusion.4 = f32[512,64]{1,0:T(8,128)S(1)} fusion(f32[512,4096]{1,0:T(8,128)} %add.36, bf16[4096,256]{1,0:T(8,128)(2,1)S(1)} %copy-done.2, s32[]{:T(128)S(6)} %select_n.24), kind=kOutput, calls=%fused_computation.7 | convolution fusion | flops 1610612736 | bytes 9568260 | tf_op jit(solution)/shard_map/dot_general | solution.py:55
  323.3 0.0 copy-done.4
  323.3 0.4 convolution_bitcast_fusion
  323.6 0.8 copy.14
  324.4 0.0 reduce-scatter.4.cloned.1.call-update
  324.4 3.2 constant_dynamic-slice_fusion
  327.6 56.0 %reduce-scatter.4.cloned.1.call-done = f32[32,64]{1,0:T(8,128)} async-done(((f32[256,64]{1,0:T(8,128)}), f32[32,64]{1,0:T(8,128)}) %reduce-scatter.4.cloned.1.call-update) | async-done | bytes 8208 | tf_op jit(solution)/shard_map/reduce_scatter | solution.py:70
  383.6 1.4 multiply_subtract_fusion
  (4 shorter events, 0.0 us)
Async XLA Ops:
  7.2 80.6 %copy-start = (bf16[1,512,512]{2,1,0:T(8,128)(2,1)S(1)}, bf16[1,512,512]{2,1,0:T(8,128)(2,1)}, u32[]{:S(2)}) copy-start(bf16[1,512,512]{2,1,0:T(8,128)(2,1)} %param.9) | copy-start | bytes 1572868
  7.2 80.6 %all-gather.3.cloned.1.call-start = ((), (), s32[]{:S(2)}) async-start(), calls=%async_computation.1 | async-start | bytes 4718592 | tf_op jit(solution)/shard_map/all_gather | solution.py:40
  7.9 162.9 %all-gather.5.cloned.1.call-start = ((), (), s32[]{:S(2)}) async-start(), calls=%async_computation.2 | async-start | bytes 2359296 | tf_op jit(solution)/shard_map/all_gather | solution.py:52
  94.8 3.2 copy-start.1
  98.1 26.1 %copy-start.3 = (f32[512,512]{1,0:T(8,128)S(1)}, f32[512,512]{1,0:T(8,128)}, u32[]{:S(2)}) copy-start(f32[512,512]{1,0:T(8,128)} %param.13) | copy-start | bytes 3145732
  98.1 26.4 %copy-start.5 = (s32[512]{0:T(512)S(1)}, s32[512]{0:T(512)}, u32[]{:S(2)}) copy-start(s32[512]{0:T(512)} %param.12) | copy-start | bytes 6148
  98.1 26.5 %copy-start.7 = (s32[2]{0:T(128)S(1)}, s32[2]{0:T(128)}, u32[]{:S(2)}) copy-start(s32[2]{0:T(128)} %param.15) | copy-start | bytes 28
  98.1 76.4 %copy-start.6 = (f32[512]{0:T(512)S(1)}, f32[512]{0:T(512)}, u32[]{:S(2)}) copy-start(f32[512]{0:T(512)} %param.14) | copy-start | bytes 6148
  98.1 13.4 %collective-permute-start = (f32[512,4096]{1,0:T(8,128)S(1)}, f32[512,4096]{1,0:T(8,128)}, u32[]{:S(2)}, u32[]{:S(2)}) collective-permute-start(f32[512,4096]{1,0:T(8,128)S(1)} %bitcast_subtract_fusion), channel_id=1, source_target_pairs={{0,8},{8,0},{16,24},{24,16},{1,9},{9,1},{17,25},{25,17},{2,10},{10... | collective-permute-start | bytes 25165832 | tf_op jit(solution)/shard_map/ppermute | solution.py:17
  122.6 182.8 %collective-permute-start.1 = (f32[512,4096]{1,0:T(8,128)}, f32[512,4096]{1,0:T(8,128)}, u32[]{:S(2)}, u32[]{:S(2)}) collective-permute-start(f32[512,4096]{1,0:T(8,128)} %add.35), channel_id=1, source_target_pairs={{0,16},{16,0},{8,24},{24,8},{1,17},{17,1},{9,25},{25,9},{2,18},{18... | collective-permute-start | bytes 25165832 | tf_op jit(solution)/shard_map/ppermute | solution.py:17
  124.1 259.5 %reduce-scatter.4.cloned.1.call-start = ((), (), s32[]{:S(2)}) async-start(), calls=%async_computation.3 | async-start | bytes 147456 | tf_op jit(solution)/shard_map/reduce_scatter | solution.py:70
  177.0 139.5 %copy-start.2 = (bf16[4096,256]{1,0:T(8,128)(2,1)S(1)}, bf16[4096,256]{1,0:T(8,128)(2,1)}, u32[]{:S(2)}) copy-start(bf16[4096,256]{1,0:T(8,128)(2,1)} %all-gather.5.cloned.1.call-done) | copy-start | bytes 6291460
  316.5 6.7 %copy-start.4 = (bf16[512,256]{1,0:T(8,128)(2,1)S(1)}, bf16[512,256]{1,0:T(8,128)(2,1)}, u32[]{:S(2)}) copy-start(bf16[512,256]{1,0:T(8,128)(2,1)} %param.11) | copy-start | bytes 786436
Sparse Core Ops, SparseCore 0:
  10.1 77.7 all-gather.2
  124.2 46.5 all-gather.4
  324.5 59.0 reduce-scatter.3
where the time goes:
time: 392 us
  waiting for transfers between devices  324 us (83%)
  other arithmetic  23.9 us (6%)
  matrix products  16.7 us (4%)
  between operations  13.9 us (4%)
  local copies, waits for them, and re-layouts  10.9 us (3%)
    ppermute x2, waiting for transfers between devices, partner(): return lax.ppermute(block, axis, route)  142 us
    all_gather x1, waiting for transfers between devices, shards(): lax.all_gather(upper_factor, 'tile', axis=2, tiled=True)  79.8 us
    reduce_scatter x1, waiting for transfers between devices, shards(): lax.psum_scatter(partial_value, 'tile', scatter_dimension=0, tiled=True)  56 us
    all_gather x1, waiting for transfers between devices, shards(): segment = lax.all_gather(modes, 'tile', axis=0, tiled=True)  46.2 us
    add x2, other arithmetic, shards(): schur_part = schur_part + partner(schur_part, 'subtree', level_bit)  22.3 us
  transfers between devices with their start and end apart: 5, of which 5 were waited for; matrix products, arithmetic and copies ran while one was open for 2% of the time, Pallas kernels for 0%

commit v1 on v0

--- a/solution.py
+++ b/solution.py
@@ -5,6 +5,20 @@
 
 SPEED_STEPS = 64
 OMEGA_TOP = 2.0
+
+
+def on_each_block(shard, axis, dim, make, out_dim):
+    ways, here, step = (lax.axis_size(axis), lax.axis_index(axis), shard.shape[dim])
+    earlier, later = ([], [])
+    going_up = going_down = shard
+    for far in range(ways // 2 + 1):
+        earlier.append(make(going_up, (here - far) % ways * step))
+        if 0 < far < ways - ways // 2:
+            later.append(make(going_down, (here + far) % ways * step))
+        going_up = lax.ppermute(going_up, axis, [(d, (d + 1) % ways) for d in range(ways)])
+        going_down = lax.ppermute(going_down, axis, [(d, (d - 1) % ways) for d in range(ways)])
+    line = jnp.concatenate([*earlier[::-1], *later], axis=out_dim)
+    return jnp.roll(line, (here - ways // 2) * earlier[0].shape[out_dim], axis=out_dim)
 
 
 def partner(block, axis, distance):
@@ -34,11 +48,14 @@
     mode_count = modes.shape[1]
     mode_cols = mode_count // branch_count
     mode_rows_dev = mode_count // tile_count
-    coupled = jnp.einsum(
-        "lrk,lkn->rn",
-        lower_factor,
-        lax.all_gather(upper_factor, "tile", axis=2, tiled=True),
-        preferred_element_type=jnp.float32,
+    coupled = on_each_block(
+        upper_factor,
+        "tile",
+        2,
+        lambda part, offset: jnp.einsum(
+            "lrk,lkn->rn", lower_factor, part, preferred_element_type=jnp.float32
+        ),
+        1,
     )
     schur_rows = jnp.sum(interface_stiffness, axis=0) - coupled
     full_width = schur_rows.shape[1]

time: 392 us -> 427 us (1.089)
  waiting for transfers between devices: 324 us -> 292 us
  starting transfers between devices: 1.67 us -> 30.5 us
  local copies, waits for them, and re-layouts: 10.9 us -> 26.8 us
  matrix products: 16.7 us -> 28.1 us
  other arithmetic: 23.9 us -> 35 us
    all_gather x1 -> x0, waiting for transfers between devices: 79.8 us -> none  [shards(): lax.all_gather(upper_factor, 'tile', axis=2, tiled=True)]
    ppermute x0 -> x7, waiting for transfers between devices: none -> 49.8 us  [the longest x4 49.8 us: on_each_block(): lax.ppermute(going_up, axis, [(d, (d + 1) % ways) for d in range(ways)])]
    ppermute x0 -> x7, starting transfers between devices: none -> 29.6 us  [the longest x3 21.5 us: on_each_block(): lax.ppermute(going_down, axis, [(d, (d - 1) % ways) for d in range(ways)])]
    unnamed x18 -> x29, local copies, waits for them, and re-layouts: 4.35 us -> 20.4 us
    sub x0 -> x1, other arithmetic: none -> 11.1 us  [shards(): schur_rows = jnp.sum(interface_stiffness, axis=0) - coupled]
    dot_general x1 -> x8, matrix products: 7.01 us -> 13.9 us  [shards(): jnp.einsum('lrk,lkn->rn', lower_factor, part, preferred_element_type=jnp....]
  transfers between devices with their start and end apart: 5 -> 11, of which waited for: 5 -> 8; matrix products, arithmetic and copies ran while one was open for 2% -> 8% of each run, Pallas kernels for 0% -> 0%
where the time goes in v1:
time: 427 us; the launch traced here: 426 us
  waiting for transfers between devices  292 us (68%)
  other arithmetic  35 us (8%)
  starting transfers between devices  30.5 us (7%)
  matrix products  28.1 us (7%)
  local copies, waits for them, and re-layouts  26.8 us (6%)
  between operations  14.2 us (3%)
    ppermute x2, waiting for transfers between devices, partner(): return lax.ppermute(block, axis, route)  139 us
    reduce_scatter x1, waiting for transfers between devices, shards(): lax.psum_scatter(partial_value, 'tile', scatter_dimension=0, tiled=True)  55.8 us
    ppermute x4, waiting for transfers between devices, on_each_block(): lax.ppermute(going_up, axis, [(d, (d + 1) % ways) for d in range(ways)])  49.8 us
    all_gather x1, waiting for transfers between devices, shards(): segment = lax.all_gather(modes, 'tile', axis=0, tiled=True)  47 us
    add x2, other arithmetic, shards(): schur_part = schur_part + partner(schur_part, 'subtree', level_bit)  22.3 us
    ppermute x3, starting transfers between devices, on_each_block(): lax.ppermute(going_down, axis, [(d, (d - 1) % ways) for d in range(ways)])  21.5 us
    unnamed x29, local copies, waits for them, and re-layouts  20.4 us
    dot_general x8, matrix products, shards(): jnp.einsum('lrk,lkn->rn', lower_factor, part, preferred_element_type=jnp....  13.9 us
  transfers between devices with their start and end apart: 11, of which 8 were waited for; matrix products, arithmetic and copies ran while one was open for 8% of the time, Pallas kernels for 0%

profile of v1, /device:TPU:0, one launch (start us, length us, event | category | flops | bytes accessed | tf_op | source)
XLA Modules:
  0.0 426.3 jit_solution(1703646700395421836)
XLA Ops:
  7.2 0.0 copy-start
  7.2 0.0 copy-start.5
  7.2 0.0 all-gather.2.cloned.1.call-start
  7.2 3.0 collective-permute-start
  10.2 15.2 %collective-permute-done = bf16[1,512,512]{2,1,0:T(8,128)(2,1)S(1)} collective-permute-done((bf16[1,512,512]{2,1,0:T(8,128)(2,1)}, bf16[1,512,512]{2,1,0:T(8,128)(2,1)S(1)}, u32[]{:S(2)}, u32[]{:S(2)}) %collective-permute-start) | collective-permute-done | bytes 524320 | tf_op jit(solution)/shard_map/ppermute | solution.py:18
  25.4 0.0 collective-permute-start.1
  25.4 4.7 %collective-permute-start.4 = (bf16[1,512,512]{2,1,0:T(8,128)(2,1)}, bf16[1,512,512]{2,1,0:T(8,128)(2,1)S(1)}, u32[]{:S(2)}, u32[]{:S(2)}) collective-permute-start(bf16[1,512,512]{2,1,0:T(8,128)(2,1)} %param.10), channel_id=1, source_target_pairs={{0,7},{1,0},{2,1},{3,2},{4,3},{5,4},{6,5},{7,6},{8,15},{9,8},{10,9... | collective-permute-start | bytes 1572872 | tf_op jit(solution)/shard_map/ppermute | solution.py:19
  30.1 17.4 %collective-permute-done.1 = bf16[1,512,512]{2,1,0:T(8,128)(2,1)S(1)} collective-permute-done((bf16[1,512,512]{2,1,0:T(8,128)(2,1)S(1)}, bf16[1,512,512]{2,1,0:T(8,128)(2,1)S(1)}, u32[]{:S(2)}, u32[]{:S(2)}) %collective-permute-start.1) | collective-permute-done | bytes 524320 | tf_op jit(solution)/shard_map/ppermute | solution.py:18
  47.5 2.5 collective-permute-start.2
  50.0 0.0 collective-permute-done.4
  50.0 12.3 %collective-permute-start.5 = (bf16[1,512,512]{2,1,0:T(8,128)(2,1)S(1)}, bf16[1,512,512]{2,1,0:T(8,128)(2,1)S(1)}, u32[]{:S(2)}, u32[]{:S(2)}) collective-permute-start(bf16[1,512,512]{2,1,0:T(8,128)(2,1)S(1)} %collective-permute-done.4), channel_id=1, source_target_pairs={{0,7},{1,0},{2,1},{3,2},{4,3},{5,4},{6,5},{7,6},{8,15},{9,8},{10,9... | collective-permute-start | bytes 1572872 | tf_op jit(solution)/shard_map/ppermute | solution.py:19
  62.4 8.9 %collective-permute-done.2 = bf16[1,512,512]{2,1,0:T(8,128)(2,1)} collective-permute-done((bf16[1,512,512]{2,1,0:T(8,128)(2,1)S(1)}, bf16[1,512,512]{2,1,0:T(8,128)(2,1)}, u32[]{:S(2)}, u32[]{:S(2)}) %collective-permute-start.2) | collective-permute-done | bytes 524320 | tf_op jit(solution)/shard_map/ppermute | solution.py:18
  71.3 2.6 collective-permute-start.3
  73.9 9.0 %copy.14 = f32[1,512,4096]{1,2,0:T(8,128)} copy(f32[1,512,4096]{2,1,0:T(8,128)} %param.8) | data formatting | bytes 16777216 | tf_op args[0]
  82.9 0.0 collective-permute-done.5
  82.9 4.5 %collective-permute-start.6 = (bf16[1,512,512]{2,1,0:T(8,128)(2,1)S(1)}, bf16[1,512,512]{2,1,0:T(8,128)(2,1)S(1)}, u32[]{:S(2)}, u32[]{:S(2)}) collective-permute-start(bf16[1,512,512]{2,1,0:T(8,128)(2,1)S(1)} %collective-permute-done.5), channel_id=1, source_target_pairs={{0,7},{1,0},{2,1},{3,2},{4,3},{5,4},{6,5},{7,6},{8,15},{9,8},{10,9... | collective-permute-start | bytes 1572872 | tf_op jit(solution)/shard_map/ppermute | solution.py:19
  87.3 8.3 %collective-permute-done.3 = bf16[1,512,512]{2,1,0:T(8,128)(2,1)} collective-permute-done((bf16[1,512,512]{2,1,0:T(8,128)(2,1)}, bf16[1,512,512]{2,1,0:T(8,128)(2,1)}, u32[]{:S(2)}, u32[]{:S(2)}) %collective-permute-start.3) | collective-permute-done | bytes 524320 | tf_op jit(solution)/shard_map/ppermute | solution.py:18
  95.6 0.0 copy-done
  95.6 2.5 constant_dynamic-update-slice_fusion.15
  98.2 2.5 constant_dynamic-update-slice_fusion.14
  100.7 1.5 constant_dynamic-update-slice_fusion.13
  102.1 1.4 constant_dynamic-update-slice_fusion.12
  103.6 0.0 copy-done.5
  103.6 1.5 constant_dynamic-update-slice_fusion.11
  105.1 1.5 constant_dynamic-update-slice_fusion.10
  106.6 1.5 constant_dynamic-update-slice_fusion.9
  108.0 0.0 collective-permute-done.6
  108.0 1.6 constant_dynamic-update-slice_fusion.8
  109.6 1.1 constant_dynamic-update-slice_fusion.7
  110.7 1.1 constant_dynamic-update-slice_fusion.6
  111.8 1.0 constant_dynamic-update-slice_fusion.5
  112.8 1.1 constant_dynamic-update-slice_fusion.4
  113.9 1.1 constant_dynamic-update-slice_fusion.3
  114.9 1.0 constant_dynamic-update-slice_fusion.2
  116.0 1.1 constant_dynamic-update-slice_fusion.1
  117.1 1.1 constant_dynamic-update-slice_fusion
  118.1 11.1 %bitcast_subtract_fusion = f32[512,4096]{0,1:T(8,128)} fusion(f32[1,512,4096]{1,2,0:T(8,128)} %copy.14, f32[512,8192]{0,1:T(8,128)} %constant_dynamic-update-slice_fusion, s32[]{:T(128)S(6)} %select_n.37), kind=kLoop, calls=%fused_computation.1 | loop fusion | flops 2097152 | bytes 25165828 | tf_op jit(solution)/shard_map/sub | solution.py:60
  129.3 0.1 collective-permute-start.7
  129.3 13.5 %collective-permute-done.7 = f32[512,4096]{0,1:T(8,128)} collective-permute-done((f32[512,4096]{0,1:T(8,128)}, f32[512,4096]{0,1:T(8,128)}, u32[]{:S(2)}, u32[]{:S(2)}) %collective-permute-start.7) | collective-permute-done | bytes 8388640 | tf_op jit(solution)/shard_map/ppermute | solution.py:31
  142.8 11.1 %add.48 = f32[512,4096]{0,1:T(8,128)} add(f32[512,4096]{0,1:T(8,128)} %bitcast_subtract_fusion, f32[512,4096]{0,1:T(8,128)} %collective-permute-done.7) | non-fusion elementwise | flops 2097152 | bytes 25165824 | tf_op jit(solution)/shard_map/add | solution.py:66
  154.0 0.6 collective-permute-start.8
  154.6 0.0 all-gather.2.cloned.1.call-update
  154.6 0.2 reduce-scatter.4.cloned.1.call-start
  154.9 0.0 copy-done.3
  154.9 1.3 copy.16
  156.2 0.0 copy-done.6
  156.2 47.0 %all-gather.2.cloned.1.call-done = bf16[4096,256]{1,0:T(8,128)(2,1)} async-done(((bf16[512,256]{1,0:T(8,128)(2,1)}), bf16[4096,256]{1,0:T(8,128)(2,1)}) %all-gather.2.cloned.1.call-update) | async-done | bytes 2097168 | tf_op jit(solution)/shard_map/all_gather | solution.py:69
  203.2 3.6 gather_fusion
  206.8 0.2 convert_select_fusion
  207.0 0.8 fusion.30
  207.8 2.6 fusion.1
  210.5 0.0 copy-start.1
  210.5 0.7 fusion.35
  211.1 125.6 %collective-permute-done.8 = f32[512,4096]{0,1:T(8,128)} collective-permute-done((f32[512,4096]{0,1:T(8,128)}, f32[512,4096]{0,1:T(8,128)}, u32[]{:S(2)}, u32[]{:S(2)}) %collective-permute-start.8) | collective-permute-done | bytes 8388640 | tf_op jit(solution)/shard_map/ppermute | solution.py:31
  336.8 11.1 %add.49 = f32[512,4096]{0,1:T(8,128)} add(f32[512,4096]{0,1:T(8,128)} %add.48, f32[512,4096]{0,1:T(8,128)} %collective-permute-done.8) | non-fusion elementwise | flops 2097152 | bytes 25165824 | tf_op jit(solution)/shard_map/add | solution.py:66
  347.9 9.6 %fusion.3 = f32[512,64]{1,0:T(8,128)S(1)} fusion(f32[512,4096]{0,1:T(8,128)} %add.49, bf16[4096,256]{1,0:T(8,128)(2,1)S(1)} %copy-done.2, s32[]{:T(128)S(6)} %select_n.39), kind=kOutput, calls=%fused_computation.6 | convolution fusion | flops 1610612736 | bytes 9568260 | tf_op jit(solution)/shard_map/dot_general | solution.py:72
  357.6 0.0 copy-done.4
  357.6 0.4 convolution_bitcast_fusion
  357.9 0.8 copy.18
  358.7 0.0 reduce-scatter.4.cloned.1.call-update
  358.7 1.8 constant_dynamic-slice_fusion
  360.5 1.8 copy.17
  362.3 55.8 %reduce-scatter.4.cloned.1.call-done = f32[32,64]{1,0:T(8,128)} async-done(((f32[256,64]{1,0:T(8,128)}), f32[32,64]{1,0:T(8,128)}) %reduce-scatter.4.cloned.1.call-update) | async-done | bytes 8208 | tf_op jit(solution)/shard_map/reduce_scatter | solution.py:87
  418.1 1.4 multiply_subtract_fusion
  (14 shorter events, 0.0 us)
Async XLA Ops:
  7.2 88.5 %copy-start = (bf16[1,512,512]{2,1,0:T(8,128)(2,1)S(1)}, bf16[1,512,512]{2,1,0:T(8,128)(2,1)}, u32[]{:S(2)}) copy-start(bf16[1,512,512]{2,1,0:T(8,128)(2,1)} %param.9) | copy-start | bytes 1572868
  7.2 96.4 %copy-start.5 = (bf16[1,512,512]{2,1,0:T(8,128)(2,1)S(1)}, bf16[1,512,512]{2,1,0:T(8,128)(2,1)}, u32[]{:S(2)}) copy-start(bf16[1,512,512]{2,1,0:T(8,128)(2,1)} %param.10) | copy-start | bytes 1572868
  7.2 196.0 %all-gather.2.cloned.1.call-start = ((), (), s32[]{:S(2)}) async-start(), calls=%async_computation.1 | async-start | bytes 2359296 | tf_op jit(solution)/shard_map/all_gather | solution.py:69
  7.2 18.2 %collective-permute-start = (bf16[1,512,512]{2,1,0:T(8,128)(2,1)}, bf16[1,512,512]{2,1,0:T(8,128)(2,1)S(1)}, u32[]{:S(2)}, u32[]{:S(2)}) collective-permute-start(bf16[1,512,512]{2,1,0:T(8,128)(2,1)} %param.10), channel_id=1, source_target_pairs={{0,1},{1,2},{2,3},{3,4},{4,5},{5,6},{6,7},{7,0},{8,9},{9,10},{10,1... | collective-permute-start | bytes 1572872 | tf_op jit(solution)/shard_map/ppermute | solution.py:18
  25.4 22.1 %collective-permute-start.1 = (bf16[1,512,512]{2,1,0:T(8,128)(2,1)S(1)}, bf16[1,512,512]{2,1,0:T(8,128)(2,1)S(1)}, u32[]{:S(2)}, u32[]{:S(2)}) collective-permute-start(bf16[1,512,512]{2,1,0:T(8,128)(2,1)S(1)} %collective-permute-done), channel_id=1, source_target_pairs={{0,1},{1,2},{2,3},{3,4},{4,5},{5,6},{6,7},{7,0},{8,9},{9,10},{10,1... | collective-permute-start | bytes 1572872 | tf_op jit(solution)/shard_map/ppermute | solution.py:18
  25.4 24.6 %collective-permute-start.4 = (bf16[1,512,512]{2,1,0:T(8,128)(2,1)}, bf16[1,512,512]{2,1,0:T(8,128)(2,1)S(1)}, u32[]{:S(2)}, u32[]{:S(2)}) collective-permute-start(bf16[1,512,512]{2,1,0:T(8,128)(2,1)} %param.10), channel_id=1, source_target_pairs={{0,7},{1,0},{2,1},{3,2},{4,3},{5,4},{6,5},{7,6},{8,15},{9,8},{10,9... | collective-permute-start | bytes 1572872 | tf_op jit(solution)/shard_map/ppermute | solution.py:19
  47.5 23.7 %collective-permute-start.2 = (bf16[1,512,512]{2,1,0:T(8,128)(2,1)S(1)}, bf16[1,512,512]{2,1,0:T(8,128)(2,1)}, u32[]{:S(2)}, u32[]{:S(2)}) collective-permute-start(bf16[1,512,512]{2,1,0:T(8,128)(2,1)S(1)} %collective-permute-done.1), channel_id=1, source_target_pairs={{0,1},{1,2},{2,3},{3,4},{4,5},{5,6},{6,7},{7,0},{8,9},{9,10},{10,1... | collective-permute-start | bytes 1572872 | tf_op jit(solution)/shard_map/ppermute | solution.py:18
  50.0 32.8 %collective-permute-start.5 = (bf16[1,512,512]{2,1,0:T(8,128)(2,1)S(1)}, bf16[1,512,512]{2,1,0:T(8,128)(2,1)S(1)}, u32[]{:S(2)}, u32[]{:S(2)}) collective-permute-start(bf16[1,512,512]{2,1,0:T(8,128)(2,1)S(1)} %collective-permute-done.4), channel_id=1, source_target_pairs={{0,7},{1,0},{2,1},{3,2},{4,3},{5,4},{6,5},{7,6},{8,15},{9,8},{10,9... | collective-permute-start | bytes 1572872 | tf_op jit(solution)/shard_map/ppermute | solution.py:19
  71.3 24.4 %collective-permute-start.3 = (bf16[1,512,512]{2,1,0:T(8,128)(2,1)}, bf16[1,512,512]{2,1,0:T(8,128)(2,1)}, u32[]{:S(2)}, u32[]{:S(2)}) collective-permute-start(bf16[1,512,512]{2,1,0:T(8,128)(2,1)} %collective-permute-done.2), channel_id=1, source_target_pairs={{0,1},{1,2},{2,3},{3,4},{4,5},{5,6},{6,7},{7,0},{8,9},{9,10},{10,1... | collective-permute-start | bytes 1572872 | tf_op jit(solution)/shard_map/ppermute | solution.py:18
  82.9 25.2 %collective-permute-start.6 = (bf16[1,512,512]{2,1,0:T(8,128)(2,1)S(1)}, bf16[1,512,512]{2,1,0:T(8,128)(2,1)S(1)}, u32[]{:S(2)}, u32[]{:S(2)}) collective-permute-start(bf16[1,512,512]{2,1,0:T(8,128)(2,1)S(1)} %collective-permute-done.5), channel_id=1, source_target_pairs={{0,7},{1,0},{2,1},{3,2},{4,3},{5,4},{6,5},{7,6},{8,15},{9,8},{10,9... | collective-permute-start | bytes 1572872 | tf_op jit(solution)/shard_map/ppermute | solution.py:19
  129.3 25.6 %copy-start.3 = (f32[512,512]{1,0:T(8,128)S(1)}, f32[512,512]{1,0:T(8,128)}, u32[]{:S(2)}) copy-start(f32[512,512]{1,0:T(8,128)} %param.13) | copy-start | bytes 3145732
  129.3 26.9 %copy-start.6 = (s32[512]{0:T(512)S(1)}, s32[512]{0:T(512)}, u32[]{:S(2)}) copy-start(s32[512]{0:T(512)} %param.12) | copy-start | bytes 6148
  129.3 26.9 %copy-start.8 = (s32[2]{0:T(128)S(1)}, s32[2]{0:T(128)}, u32[]{:S(2)}) copy-start(s32[2]{0:T(128)} %param.15) | copy-start | bytes 28
  129.3 77.7 %copy-start.7 = (f32[512]{0:T(512)S(1)}, f32[512]{0:T(512)}, u32[]{:S(2)}) copy-start(f32[512]{0:T(512)} %param.14) | copy-start | bytes 6148
  129.3 13.6 %collective-permute-start.7 = (f32[512,4096]{0,1:T(8,128)}, f32[512,4096]{0,1:T(8,128)}, u32[]{:S(2)}, u32[]{:S(2)}) collective-permute-start(f32[512,4096]{0,1:T(8,128)} %bitcast_subtract_fusion), channel_id=1, source_target_pairs={{0,8},{8,0},{16,24},{24,16},{1,9},{9,1},{17,25},{25,17},{2,10},{10... | collective-permute-start | bytes 25165832 | tf_op jit(solution)/shard_map/ppermute | solution.py:31
  154.0 182.8 %collective-permute-start.8 = (f32[512,4096]{0,1:T(8,128)}, f32[512,4096]{0,1:T(8,128)}, u32[]{:S(2)}, u32[]{:S(2)}) collective-permute-start(f32[512,4096]{0,1:T(8,128)} %add.48), channel_id=1, source_target_pairs={{0,16},{16,0},{8,24},{24,8},{1,17},{17,1},{9,25},{25,9},{2,18},{18... | collective-permute-start | bytes 25165832 | tf_op jit(solution)/shard_map/ppermute | solution.py:31
  154.6 263.4 %reduce-scatter.4.cloned.1.call-start = ((), (), s32[]{:S(2)}) async-start(), calls=%async_computation.2 | async-start | bytes 147456 | tf_op jit(solution)/shard_map/reduce_scatter | solution.py:87
  203.2 144.7 %copy-start.2 = (bf16[4096,256]{1,0:T(8,128)(2,1)S(1)}, bf16[4096,256]{1,0:T(8,128)(2,1)}, u32[]{:S(2)}) copy-start(bf16[4096,256]{1,0:T(8,128)(2,1)} %all-gather.2.cloned.1.call-done) | copy-start | bytes 6291460
  210.5 209.0 %copy-start.1 = (bf16[1,512,512]{2,1,0:T(8,128)(2,1)S(1)}, bf16[1,512,512]{2,1,0:T(8,128)(2,1)}, u32[]{:S(2)}) copy-start(bf16[1,512,512]{2,1,0:T(8,128)(2,1)} %param.9) | copy-start | bytes 1572868
  211.1 146.4 %copy-start.4 = (bf16[512,256]{1,0:T(8,128)(2,1)S(1)}, bf16[512,256]{1,0:T(8,128)(2,1)}, u32[]{:S(2)}) copy-start(bf16[512,256]{1,0:T(8,128)(2,1)} %param.11) | copy-start | bytes 786436
Sparse Core Ops, SparseCore 0:
  154.7 48.4 all-gather.1
  358.8 59.1 reduce-scatter.3
